TPU v7x, 32 devices: a whole 2x2x4 slice. The times are simulated.
32 devices in a mesh: dp: 8 (over z, x), band: 4 (over y, core).
Axes of the slice: x: 2, y: 2, z: 4, core: 2. Of those that a mesh axis runs over, the one named last changes fastest.
Arguments:
- inputs: bfloat16 [2, 8, 2048, 768], P(None, 'dp', 'band'), may hold values from -6 to 6
- segments: int32 [2, 8, 2048], P(None, 'dp', 'band'), may hold values from 0 to 6, as said below
- cotangent: bfloat16 [2, 8, 2048, 768], P(None, 'dp', 'band'), may hold values from -6 to 6
- ln1_gain: bfloat16 [768], P('band'), may hold values from 0.5 to 1.5
- ln1_bias: bfloat16 [768], P('band'), may hold values from -3 to 3
- w_qkv: bfloat16 [768, 2304], P('band'), may hold values from -0.21875 to 0.21875
- b_qv: bfloat16 [1536], P('band'), may hold values from -0.4375 to 0.4375
- w_out: bfloat16 [768, 768], P('band'), may hold values from -2.5 to 2.5
- b_out: bfloat16 [768], P('band'), may hold values from -3 to 3
- ln2_gain: bfloat16 [768], P('band'), may hold values from 0.5 to 1.5
- ln2_bias: bfloat16 [768], P('band'), may hold values from -3 to 3
- w_up: bfloat16 [768, 3072], P('band'), may hold values from -0.21875 to 0.21875
- b_up: bfloat16 [3072], P('band'), may hold values from -3 to 3
- w_down: bfloat16 [3072, 768], P('band'), may hold values from -0.109375 to 0.109375
- b_down: bfloat16 [768], P('band'), may hold values from -3 to 3
Outputs:
- output: bfloat16 [2, 8, 2048, 768], P(None, 'dp', 'band')
- input_grad: bfloat16 [2, 8, 2048, 768], P(None, 'dp', 'band')
- grad_ln1_gain: float32 [768], P('band')
- grad_ln1_bias: float32 [768], P('band')
- grad_w_qkv: float32 [768, 2304], P('band')
- grad_b_qv: float32 [1536], P('band')
- grad_w_out: float32 [768, 768], P('band')
- grad_b_out: float32 [768], P('band')
- grad_ln2_gain: float32 [768], P('band')
- grad_ln2_bias: float32 [768], P('band')
- grad_w_up: float32 [768, 3072], P('band')
- grad_b_up: float32 [3072], P('band')
- grad_w_down: float32 [3072, 768], P('band')
- grad_b_down: float32 [768], P('band')
Inputs may be any that keep to these rules, and one draw needn't show every extreme that they name: `segments`: each sequence's 2048 slots are consecutive blocks of 512 slots that carry the same ids in the same order. In a block, ids never fall: tiles 1, 2, 3 and so on are contiguous runs, and padding (0) fills the end of the block, at most 51 slots.
All inputs are finite; a program needn't handle non-finite values.
Results may differ from a plain program's by a relative error of at most 0.02.
Values may be sent and summed in bfloat16 or wider, within the bound.
No kernel may reach another device: no remote copies, remote signals or barrier semaphores. Data moves between devices by JAX's collectives and lax.ppermute only.
A program may use at most 192 MiB of HBM per device.

v0:
```python
import jax
import jax.numpy as jnp
from jax import lax
from jax.sharding import PartitionSpec as P

HD = 64
D = 768


def inner_dot(left, right):
    return jnp.dot(left, right, preferred_element_type=jnp.float32)


def row_dot(left, right):
    return lax.dot_general(
        left, right, (((0,), (0,)), ((), ())), preferred_element_type=jnp.float32
    )


def col_dot(left, right):
    return lax.dot_general(
        left, right, (((1,), (1,)), ((), ())), preferred_element_type=jnp.float32
    )


def normed(value, gain, shift):
    center = value - jnp.mean(value, axis=-1, keepdims=True)
    spread = jnp.mean(center * center, axis=-1, keepdims=True)
    return center * lax.rsqrt(spread + 1e-06) * gain + shift


def gelu_tanh(value):
    return jax.nn.gelu(value, approximate=True)


def split_heads(block, heads):
    return block.reshape(block.shape[0], heads, -1).transpose(1, 0, 2)


def merge_heads(block):
    return block.transpose(1, 0, 2).reshape(block.shape[1], -1)


def blocks_of(array, count):
    return array.reshape((count, array.shape[0] // count) + array.shape[1:])


def masked_scores(query, keys, seg_query, seg_keys):
    scores = col_dot(query, keys) * 0.125
    return jnp.where(seg_query[:, None] == seg_keys[None, :], scores, -1e30)


def attend_forward(query, keys, values, seg_query, seg_keys, count):

    def per_head(item):
        head_query, head_keys, head_values = item

        def per_block(piece):
            block_query, block_seg = piece
            scores = masked_scores(block_query, head_keys, block_seg, seg_keys)
            peak = jnp.max(scores, axis=-1, keepdims=True)
            raised = jnp.exp(scores - peak)
            total = jnp.sum(raised, axis=-1, keepdims=True)
            weights = (raised / total).astype(jnp.bfloat16)
            return (inner_dot(weights, head_values), (peak + jnp.log(total))[:, 0])

        result, log_total = lax.map(
            per_block, (blocks_of(head_query, count), blocks_of(seg_query, count))
        )
        return (result.reshape(head_query.shape), log_total.reshape(-1))

    return lax.map(per_head, (query, keys, values))


def attend_backward(query, keys, values, grad_out, log_total, seg_query, seg_keys, count):

    def per_head(item):
        head_query, head_keys, head_values, head_grad, head_total = item

        def per_block(carry, piece):
            grad_keys, grad_values = carry
            block_query, block_grad, block_total, block_seg = piece
            scores = masked_scores(block_query, head_keys, block_seg, seg_keys)
            weights = jnp.exp(scores - block_total[:, None])
            grad_values = grad_values + row_dot(weights.astype(jnp.bfloat16), block_grad)
            grad_weights = col_dot(block_grad, head_values)
            center = jnp.sum(weights * grad_weights, axis=-1, keepdims=True)
            grad_scores = (weights * (grad_weights - center)).astype(jnp.bfloat16)
            grad_query = inner_dot(grad_scores, head_keys) * 0.125
            grad_keys = grad_keys + row_dot(grad_scores, block_query) * 0.125
            return ((grad_keys, grad_values), grad_query)

        start = jnp.zeros(head_keys.shape, jnp.float32)
        (grad_keys, grad_values), grad_query = lax.scan(
            per_block,
            (start, start),
            (
                blocks_of(head_query, count),
                blocks_of(head_grad, count),
                blocks_of(head_total, count),
                blocks_of(seg_query, count),
            ),
        )
        return (grad_query.reshape(head_query.shape), grad_keys, grad_values)

    return lax.map(per_head, (query, keys, values, grad_out, log_total))


def layer_pass(inputs, segment, cotangent, whole, parts):
    (
        gain_one,
        shift_one,
        w_proj,
        b_proj,
        w_mix,
        b_mix,
        gain_two,
        shift_two,
        w_rise,
        b_rise,
        w_fall,
        b_fall,
    ) = whole
    gain_one = gain_one.astype(jnp.float32)
    shift_one = shift_one.astype(jnp.float32)
    gain_two = gain_two.astype(jnp.float32)
    shift_two = shift_two.astype(jnp.float32)
    b_proj = b_proj.astype(jnp.float32)
    b_mix = b_mix.astype(jnp.float32)
    b_rise = b_rise.astype(jnp.float32)
    b_fall = b_fall.astype(jnp.float32)
    heads = D // HD
    count = max(inputs.shape[0] // 512, 1)
    value = inputs.astype(jnp.float32)
    normed_in, pull_one = jax.vjp(normed, value, gain_one, shift_one)
    normed_low = normed_in.astype(jnp.bfloat16)
    projected = inner_dot(normed_low, w_proj)
    query = (projected[:, :D] + b_proj[:D]).astype(jnp.bfloat16)
    key_part = projected[:, D : 2 * D].astype(jnp.bfloat16)
    value_part = (projected[:, 2 * D :] + b_proj[D:]).astype(jnp.bfloat16)
    keys_all, values_all = (
        lax.all_gather(key_part, "band", axis=0, tiled=True),
        lax.all_gather(value_part, "band", axis=0, tiled=True),
    )
    seg_keys = jnp.tile(segment, parts)
    query_heads = split_heads(query, heads)
    keys_heads = split_heads(keys_all, heads)
    values_heads = split_heads(values_all, heads)
    head_out, log_total = attend_forward(
        query_heads, keys_heads, values_heads, segment, seg_keys, count
    )
    mixed = merge_heads(head_out).astype(jnp.bfloat16)
    hidden = value + (inner_dot(mixed, w_mix) + b_mix)
    normed_mid, pull_two = jax.vjp(normed, hidden, gain_two, shift_two)
    mid_low = normed_mid.astype(jnp.bfloat16)
    upward = inner_dot(mid_low, w_rise) + b_rise
    active, pull_gelu = jax.vjp(gelu_tanh, upward)
    active_low = active.astype(jnp.bfloat16)
    output = hidden + (inner_dot(active_low, w_fall) + b_fall)
    grad_y = cotangent.astype(jnp.float32) * (segment != 0).astype(jnp.float32)[:, None]
    grad_m = grad_y.astype(jnp.bfloat16)
    grad_w_fall = row_dot(active_low, grad_m)
    grad_b_fall = jnp.sum(grad_m.astype(jnp.float32), axis=0)
    grad_up = pull_gelu(col_dot(grad_m, w_fall))[0].astype(jnp.bfloat16)
    grad_w_rise = row_dot(mid_low, grad_up)
    grad_b_rise = jnp.sum(grad_up.astype(jnp.float32), axis=0)
    grad_mid, grad_gain_two, grad_shift_two = pull_two(col_dot(grad_up, w_rise))
    grad_hidden = grad_y + grad_mid
    grad_a = grad_hidden.astype(jnp.bfloat16)
    grad_w_mix = row_dot(mixed, grad_a)
    grad_b_mix = jnp.sum(grad_a.astype(jnp.float32), axis=0)
    grad_mixed = col_dot(grad_a, w_mix).astype(jnp.bfloat16)
    grad_heads = split_heads(grad_mixed, heads)
    grad_query, grad_keys, grad_values = attend_backward(
        query_heads, keys_heads, values_heads, grad_heads, log_total, segment, seg_keys, count
    )
    keys_sum, values_sum = (
        lax.psum_scatter(
            merge_heads(grad_keys).astype(jnp.bfloat16), "band", scatter_dimension=0, tiled=True
        ).astype(jnp.float32),
        lax.psum_scatter(
            merge_heads(grad_values).astype(jnp.bfloat16), "band", scatter_dimension=0, tiled=True
        ).astype(jnp.float32),
    )
    query_low = merge_heads(grad_query).astype(jnp.bfloat16)
    values_low = values_sum.astype(jnp.bfloat16)
    grad_qkv = jnp.concatenate([query_low, keys_sum.astype(jnp.bfloat16), values_low], axis=1)
    grad_w_proj = row_dot(normed_low, grad_qkv)
    grad_b_proj = jnp.concatenate(
        [
            jnp.sum(query_low.astype(jnp.float32), axis=0),
            jnp.sum(values_low.astype(jnp.float32), axis=0),
        ]
    )
    grad_norm_in, grad_gain_one, grad_shift_one = pull_one(col_dot(grad_qkv, w_proj))
    grad_input = grad_hidden + grad_norm_in
    grads = (
        grad_gain_one,
        grad_shift_one,
        grad_w_proj,
        grad_b_proj,
        grad_w_mix,
        grad_b_mix,
        grad_gain_two,
        grad_shift_two,
        grad_w_rise,
        grad_b_rise,
        grad_w_fall,
        grad_b_fall,
    )
    return (output.astype(jnp.bfloat16), grad_input.astype(jnp.bfloat16), grads)


def gather_each(shards):
    return (
        lax.all_gather(shards[0], "band", axis=0, tiled=True),
        lax.all_gather(shards[1], "band", axis=0, tiled=True),
        lax.all_gather(shards[2], "band", axis=0, tiled=True),
        lax.all_gather(shards[3], "band", axis=0, tiled=True),
        lax.all_gather(shards[4], "band", axis=0, tiled=True),
        lax.all_gather(shards[5], "band", axis=0, tiled=True),
        lax.all_gather(shards[6], "band", axis=0, tiled=True),
        lax.all_gather(shards[7], "band", axis=0, tiled=True),
        lax.all_gather(shards[8], "band", axis=0, tiled=True),
        lax.all_gather(shards[9], "band", axis=0, tiled=True),
        lax.all_gather(shards[10], "band", axis=0, tiled=True),
        lax.all_gather(shards[11], "band", axis=0, tiled=True),
    )


def reduce_end(grads):
    shares = (
        lax.psum_scatter(
            grads[0].astype(jnp.bfloat16), "band", scatter_dimension=0, tiled=True
        ).astype(jnp.float32),
        lax.psum_scatter(
            grads[1].astype(jnp.bfloat16), "band", scatter_dimension=0, tiled=True
        ).astype(jnp.float32),
        lax.psum_scatter(
            grads[2].astype(jnp.bfloat16), "band", scatter_dimension=0, tiled=True
        ).astype(jnp.float32),
        lax.psum_scatter(
            grads[3].astype(jnp.bfloat16), "band", scatter_dimension=0, tiled=True
        ).astype(jnp.float32),
        lax.psum_scatter(
            grads[4].astype(jnp.bfloat16), "band", scatter_dimension=0, tiled=True
        ).astype(jnp.float32),
        lax.psum_scatter(
            grads[5].astype(jnp.bfloat16), "band", scatter_dimension=0, tiled=True
        ).astype(jnp.float32),
        lax.psum_scatter(
            grads[6].astype(jnp.bfloat16), "band", scatter_dimension=0, tiled=True
        ).astype(jnp.float32),
        lax.psum_scatter(
            grads[7].astype(jnp.bfloat16), "band", scatter_dimension=0, tiled=True
        ).astype(jnp.float32),
        lax.psum_scatter(
            grads[8].astype(jnp.bfloat16), "band", scatter_dimension=0, tiled=True
        ).astype(jnp.float32),
        lax.psum_scatter(
            grads[9].astype(jnp.bfloat16), "band", scatter_dimension=0, tiled=True
        ).astype(jnp.float32),
        lax.psum_scatter(
            grads[10].astype(jnp.bfloat16), "band", scatter_dimension=0, tiled=True
        ).astype(jnp.float32),
        lax.psum_scatter(
            grads[11].astype(jnp.bfloat16), "band", scatter_dimension=0, tiled=True
        ).astype(jnp.float32),
    )
    return (
        lax.psum(shares[0].astype(jnp.bfloat16), "dp").astype(jnp.float32),
        lax.psum(shares[1].astype(jnp.bfloat16), "dp").astype(jnp.float32),
        lax.psum(shares[2].astype(jnp.bfloat16), "dp").astype(jnp.float32),
        lax.psum(shares[3].astype(jnp.bfloat16), "dp").astype(jnp.float32),
        lax.psum(shares[4].astype(jnp.bfloat16), "dp").astype(jnp.float32),
        lax.psum(shares[5].astype(jnp.bfloat16), "dp").astype(jnp.float32),
        lax.psum(shares[6].astype(jnp.bfloat16), "dp").astype(jnp.float32),
        lax.psum(shares[7].astype(jnp.bfloat16), "dp").astype(jnp.float32),
        lax.psum(shares[8].astype(jnp.bfloat16), "dp").astype(jnp.float32),
        lax.psum(shares[9].astype(jnp.bfloat16), "dp").astype(jnp.float32),
        lax.psum(shares[10].astype(jnp.bfloat16), "dp").astype(jnp.float32),
        lax.psum(shares[11].astype(jnp.bfloat16), "dp").astype(jnp.float32),
    )


def body(
    inputs,
    segments,
    cotangent,
    ln1_gain,
    ln1_bias,
    w_qkv,
    b_qv,
    w_out,
    b_out,
    ln2_gain,
    ln2_bias,
    w_up,
    b_up,
    w_down,
    b_down,
):
    shards = (
        ln1_gain,
        ln1_bias,
        w_qkv,
        b_qv,
        w_out,
        b_out,
        ln2_gain,
        ln2_bias,
        w_up,
        b_up,
        w_down,
        b_down,
    )
    parts = lax.axis_size("band")
    results = []
    grads_in = []
    totals = None
    for batch in range(inputs.shape[0]):
        whole = gather_each(shards)
        result, grad_in, grads = layer_pass(
            inputs[batch, 0], segments[batch, 0], cotangent[batch, 0], whole, parts
        )
        totals = (
            grads
            if totals is None
            else tuple((first + second for first, second in zip(totals, grads)))
        )
        results.append(result)
        grads_in.append(grad_in)
    totals = reduce_end(totals)
    return (jnp.stack(results)[:, None], jnp.stack(grads_in)[:, None]) + tuple(totals)


def solution(mesh):
    return jax.shard_map(
        body,
        mesh=mesh,
        in_specs=(
            P(None, "dp", "band", None),
            P(None, "dp", "band"),
            P(None, "dp", "band", None),
            P("band"),
            P("band"),
            P("band", None),
            P("band"),
            P("band", None),
            P("band"),
            P("band"),
            P("band"),
            P("band", None),
            P("band"),
            P("band", None),
            P("band"),
        ),
        out_specs=(
            P(None, "dp", "band", None),
            P(None, "dp", "band", None),
            P("band"),
            P("band"),
            P("band", None),
            P("band"),
            P("band", None),
            P("band"),
            P("band"),
            P("band"),
            P("band", None),
            P("band"),
            P("band", None),
            P("band"),
        ),
        check_vma=False,
    )
```

profile of v0, /device:TPU:0, one launch (start us, length us, event | category | flops | bytes accessed | tf_op | source)
XLA Modules:
  0.0 1097.1 jit_solution(7388853677042379467)
XLA Ops:
  14.2 13.5 %all-reduce.17 = (bf16[768]{0:T(1024)(128)(2,1)S(1)}, bf16[768]{0:T(1024)(128)(2,1)S(1)}, bf16[768]{0:T(1024)(128)(2,1)S(1)}, bf16[768]{0:T(1024)(128)(2,1)S(1)}, bf16[768]{0:T(1024)(128)(2,1)S(1)}) all-reduce(bf16[768]{0:T(1024)(128)(2,1)S(1)} %dynamic-update-slice.1, ...), channel_id=1, replica_groups=mesh['dp'=8,'band'=4] {'band'}, use_global_device_ids=true, to_apply=%add.1 | all-reduce | flops 3840 | bytes 15360
  73.9 7.5 all-gather.25.cloned.1.call-done
  86.2 6.7 copy.74
  93.0 19.2 %all-gather.23.cloned.1.call-done = bf16[2048,768]{1,0:T(8,128)(2,1)} async-done(((bf16[512,768]{1,0:T(8,128)(2,1)}), bf16[2048,768]{1,0:T(8,128)(2,1)}) %all-gather.23.cloned.1.call-update) | async-done | bytes 3145744 | tf_op jit(solution)/shard_map/all_gather | solution.py:142
  116.9 6.7 copy.73
  124.6 104.7 %while.51 = (s32[]{:T(128)}, bf16[12,512,64]{1,2,0:T(8,128)(2,1)}, f32[12,512]{1,0:T(8,128)S(1)}, s32[1,1,512]{2,1,0:T(1,128)S(1)}, bf16[12,512,64]{2,1,0:T(8,12...) while((s32[]{:T(128)}, bf16[12,512,64]{1,2,0:T(8,128)(2,1)}, ...), condition=%wide.region_13.14_spmd.clone, body=%wide.region_10.13_spmd.clone.sunk | while | flops 277872128 | bytes 30730372 | solution.py:72
  252.7 97.4 %while.50 = (s32[]{:T(128)}, bf16[12,512,64]{1,2,0:T(8,128)(2,1)S(1)}, f32[12,512]{1,0:T(8,128)S(1)}, s32[1,1,512]{2,1,0:T(1,128)S(1)}, bf16[12,512,64]{2,1,0:T(...) while((s32[]{:T(128)}, ...), condition=%wide.region_5.6_spmd.clone, body=%wide.region_2.5_spmd.clone.sunk | while | flops 277872128 | bytes 30730372 | solution.py:72
  356.3 7.3 fusion.171
  368.6 9.7 convert_reduce_fusion.1
  385.1 8.8 convert_reduce_fusion
  407.9 130.6 %while.52 = (s32[]{:T(128)}, bf16[12,512,64]{1,2,0:T(8,128)(2,1)}, bf16[12,2048,64]{1,2,0:T(8,128)(2,1)S(1)}, bf16[12,2048,64]{1,2,0:T(8,128)(2,1)}, s32[1,1,512...) while((s32[]{:T(128)}, bf16[12,512,64]{1,2,0:T(8,128)(2,1)}, ...), condition=%wide.region_20.21_spmd.clone, body=%wide.region_18.20_spmd.clone.sunk | while | flops 681737728 | bytes 34655352 | solution.py:106
  548.6 139.4 %while.53 = (s32[]{:T(128)}, bf16[12,512,64]{1,2,0:T(8,128)(2,1)}, bf16[12,2048,64]{1,2,0:T(8,128)(2,1)S(1)}, bf16[12,2048,64]{1,2,0:T(8,128)(2,1)}, s32[1,1,512...) while((s32[]{:T(128)}, bf16[12,512,64]{1,2,0:T(8,128)(2,1)}, ...), condition=%wide.region_29.30_spmd.clone, body=%wide.region_27.29_spmd.clone.sunk | while | flops 681737728 | bytes 34655352 | solution.py:106
  700.2 9.0 add_convert_fusion
  721.6 6.9 fusion.135
  728.5 39.2 %reduce-scatter.15.cloned.1.call-done = bf16[512,768]{0,1:T(8,128)(2,1)} async-done(((bf16[2048,768]{0,1:T(8,128)(2,1)}), bf16[512,768]{0,1:T(8,128)(2,1)}) %reduce-scatter.15.cloned.1.call-update) | async-done | bytes 786448 | tf_op jit(solution)/shard_map/reduce_scatter | solution.py:181
  767.7 7.9 add_convert_fusion.2
  796.5 50.4 %reduce-scatter.23.cloned.1.call-done = bf16[768,768]{1,0:T(8,128)(2,1)} async-done(((bf16[3072,768]{1,0:T(8,128)(2,1)}), bf16[768,768]{1,0:T(8,128)(2,1)}) %reduce-scatter.23.cloned.1.call-update) | async-done | bytes 1179664 | tf_op jit(solution)/shard_map/reduce_scatter | solution.py:263
  846.9 50.4 %reduce-scatter.21.cloned.1.call-done = bf16[192,3072]{1,0:T(8,128)(2,1)} async-done(((bf16[768,3072]{1,0:T(8,128)(2,1)}), bf16[192,3072]{1,0:T(8,128)(2,1)}) %reduce-scatter.21.cloned.1.call-update) | async-done | bytes 1179664 | tf_op jit(solution)/shard_map/reduce_scatter | solution.py:257
  897.3 42.8 %reduce-scatter.17.cloned.1.call-done = bf16[192,2304]{1,0:T(8,128)(2,1)} async-done(((bf16[768,2304]{1,0:T(8,128)(2,1)}), bf16[192,2304]{1,0:T(8,128)(2,1)}) %reduce-scatter.17.cloned.1.call-update) | async-done | bytes 884752 | tf_op jit(solution)/shard_map/reduce_scatter | solution.py:239
  941.5 10.5 all-reduce.16
  952.6 23.1 %all-reduce.14 = (bf16[192]{0:T(256)(128)(2,1)S(1)}, bf16[192]{0:T(256)(128)(2,1)S(1)}, bf16[384]{0:T(512)(128)(2,1)S(1)}, bf16[192]{0:T(256)(128)(2,1)S(1)}, bf...) all-reduce(bf16[192]{0:T(256)(128)(2,1)S(1)} %dynamic-slice.7, ...), channel_id=1, replica_groups=mesh['dp'=8,'band'=4] {'dp'}, use_global_device_ids=true, to_apply=%region_37.38 | all-reduce | flops 2304 | bytes 9216 | tf_op jit(solution)/shard_map/psum | solution.py:271
  984.6 8.3 fusion.132
  992.9 8.3 fusion.133
  1002.5 81.1 %all-reduce.20.cloned.1.call-done = (bf16[192,2304]{1,0:T(8,128)(2,1)}, bf16[192,768]{1,0:T(8,128)(2,1)}, bf16[192,3072]{1,0:T(8,128)(2,1)}, bf16[768,768]{1,0:T(8,128)(2,1)}) async-done(((bf16[192,2304]{1,0:T(8,128)(2,1)}, bf16[192,768]{1,0:T(8,128)(2,1)}, bf16[192,3072]{1,0:T(8,128)(2,1)}, bf16[768,768]{1,0:T(8,128)(2,1)}), (bf16[192,2304]{1,0:T(8,128)(2,1)}, bf16[192,768]{1,0:T(8,128)(2,1)}, ...) | async-done | bytes 3538960 | tf_op jit(solution)/shard_map/psum | solution.py:273
  (773 shorter events, 660.0 us)
Async XLA Ops:
  7.2 28.2 %copy-start.2 = (bf16[2,1,512,768]{3,2,1,0:T(8,128)(2,1)S(1)}, bf16[2,1,512,768]{3,2,1,0:T(8,128)(2,1)}, u32[]{:S(2)}) copy-start(bf16[2,1,512,768]{3,2,1,0:T(8,128)(2,1)} %param.23) | copy-start | bytes 4718596
  7.2 36.0 %all-gather.11.cloned.1.call-start = ((), (), s32[]{:S(2)}) async-start(), calls=%async_computation.8 | async-start | bytes 4423680 | tf_op jit(solution)/shard_map/all_gather | solution.py:218
  7.9 73.6 %all-gather.25.cloned.1.call-start = ((), (), s32[]{:S(2)}) async-start(), calls=%async_computation.15 | async-start | bytes 3932160 | tf_op jit(solution)/shard_map/all_gather | solution.py:143
  52.7 59.5 %all-gather.23.cloned.1.call-start = ((), (), s32[]{:S(2)}) async-start(), calls=%async_computation.14 | async-start | bytes 3932160 | tf_op jit(solution)/shard_map/all_gather | solution.py:142
  55.1 174.1 %all-gather.15.cloned.1.call-start = ((), (), s32[]{:S(2)}) async-start(), calls=%async_computation.10 | async-start | bytes 3932160 | tf_op jit(solution)/shard_map/all_gather | solution.py:143
  55.8 185.5 %all-gather.13.cloned.1.call-start = ((), (), s32[]{:S(2)}) async-start(), calls=%async_computation.9 | async-start | bytes 3932160 | tf_op jit(solution)/shard_map/all_gather | solution.py:142
  58.2 291.9 %all-gather.17.cloned.1.call-start = ((), (), s32[]{:S(2)}) async-start(), calls=%async_computation.11 | async-start | bytes 1474560 | tf_op jit(solution)/shard_map/all_gather | solution.py:220
  58.8 297.5 %all-gather.19.cloned.1.call-start = ((), (), s32[]{:S(2)}) async-start(), calls=%async_computation.12 | async-start | bytes 5898240 | tf_op jit(solution)/shard_map/all_gather | solution.py:224
  59.5 309.1 %all-gather.21.cloned.1.call-start = ((), (), s32[]{:S(2)}) async-start(), calls=%async_computation.13 | async-start | bytes 5898240 | tf_op jit(solution)/shard_map/all_gather | solution.py:226
  60.3 660.2 %reduce-scatter.11.cloned.1.call-start = ((), (), s32[]{:S(2)}) async-start(), calls=%async_computation.17 | async-start | bytes 3932160 | tf_op jit(solution)/shard_map/reduce_scatter | solution.py:181
  60.4 303.2 %copy-start.62 = (f32[768]{0:T(1024)}, f32[768]{0:T(1024)S(1)}, u32[]{:S(2)}) copy-start(f32[768]{0:T(1024)S(1)} %convert_element_type.389) | copy-start | bytes 9220
  353.6 44.2 %copy-start.13 = (f32[512,768]{1,0:T(8,128)}, f32[512,768]{1,0:T(8,128)S(1)}, u32[]{:S(2)}) copy-start(f32[512,768]{1,0:T(8,128)S(1)} %get-tuple-element.709) | copy-start | bytes 4718596
  538.5 182.0 %reduce-scatter.9.cloned.1.call-start = ((), (), s32[]{:S(2)}) async-start(), calls=%async_computation.16 | async-start | bytes 3932160 | tf_op jit(solution)/shard_map/reduce_scatter | solution.py:178
  545.1 183.3 %reduce-scatter.13.cloned.1.call-start = ((), (), s32[]{:S(2)}) async-start(), calls=%async_computation.18 | async-start | bytes 3932160 | tf_op jit(solution)/shard_map/reduce_scatter | solution.py:178
  689.7 78.0 %reduce-scatter.15.cloned.1.call-start = ((), (), s32[]{:S(2)}) async-start(), calls=%async_computation.19 | async-start | bytes 3932160 | tf_op jit(solution)/shard_map/reduce_scatter | solution.py:181
  690.3 106.2 %reduce-scatter.19.cloned.1.call-start = ((), (), s32[]{:S(2)}) async-start(), calls=%async_computation.21 | async-start | bytes 1474560 | tf_op jit(solution)/shard_map/reduce_scatter | solution.py:245
  693.7 153.2 %reduce-scatter.23.cloned.1.call-start = ((), (), s32[]{:S(2)}) async-start(), calls=%async_computation.23 | async-start | bytes 5898240 | tf_op jit(solution)/shard_map/reduce_scatter | solution.py:263
  709.2 188.0 %reduce-scatter.21.cloned.1.call-start = ((), (), s32[]{:S(2)}) async-start(), calls=%async_computation.22 | async-start | bytes 5898240 | tf_op jit(solution)/shard_map/reduce_scatter | solution.py:257
  720.2 219.9 %reduce-scatter.17.cloned.1.call-start = ((), (), s32[]{:S(2)}) async-start(), calls=%async_computation.20 | async-start | bytes 4423680 | tf_op jit(solution)/shard_map/reduce_scatter | solution.py:239
  721.6 46.1 %copy-start.41 = (f32[512]{0:T(512)S(1)}, f32[512]{0:T(512)}, u32[]{:S(2)}) copy-start(f32[512]{0:T(512)} %copy-done.40) | copy-start | bytes 6148
  721.6 46.1 %copy-start.45 = (f32[512]{0:T(512)S(1)}, f32[512]{0:T(512)}, u32[]{:S(2)}) copy-start(f32[512]{0:T(512)} %copy-done.44) | copy-start | bytes 6148
  775.6 307.9 %all-reduce.20.cloned.1.call-start = ((), (), s32[]{:S(2)}) async-start(), calls=%async_computation.24 | async-start | bytes 7077888 | tf_op jit(solution)/shard_map/psum | solution.py:273
  795.3 185.0 %copy-start.5 = (f32[512,768]{1,0:T(8,128)S(1)}, f32[512,768]{1,0:T(8,128)}, u32[]{:S(2)}) copy-start(f32[512,768]{1,0:T(8,128)} %copy-done.4) | copy-start | bytes 4718596
  795.3 185.0 %copy-start.49 = (f32[512]{0:T(512)S(1)}, f32[512]{0:T(512)}, u32[]{:S(2)}) copy-start(f32[512]{0:T(512)} %copy-done.48) | copy-start | bytes 6148
  (99 other events, 398.7 us)
Sparse Core Ops, SparseCore 0:
  9.6 33.6 all-gather.10
  52.8 28.6 all-gather.24
  83.6 28.4 all-gather.22
  114.2 28.5 all-gather.14
  144.1 28.5 all-gather.12
  174.1 17.4 all-gather.16
  193.1 37.4 all-gather.18
  232.1 37.4 all-gather.20
  538.6 37.8 reduce-scatter.10
  578.8 37.7 reduce-scatter.8
  689.8 37.6 reduce-scatter.12
  729.9 37.7 reduce-scatter.14
  770.8 25.6 reduce-scatter.18
  798.9 47.9 reduce-scatter.22
  849.3 47.9 reduce-scatter.20
  899.7 40.3 reduce-scatter.16
  943.9 139.5 all-reduce.19
where the time goes:
time: 1110 us; the launch traced here: 1100 us
  matrix products  508 us (46%)
  waiting for transfers between devices  302 us (27%)
  local copies, waits for them, and re-layouts  147 us (13%)
  other arithmetic  61.3 us (6%)
  blocking collectives  57.8 us (5%)
  between operations  18 us (2%)
    dot_general x80, matrix products, col_dot(): lax.dot_general(left, right, (((1,), (1,)), ((), ())), preferred_element_...  197 us
    dot_general x56, matrix products, inner_dot(): return jnp.dot(left, right, preferred_element_type=jnp.float32)  184 us
    dot_general x56, matrix products, row_dot(): lax.dot_general(left, right, (((0,), (0,)), ((), ())), preferred_element_...  127 us
    psum x1, waiting for transfers between devices, reduce_end(): lax.psum(shares[2].astype(jnp.bfloat16), 'dp').astype(jnp.float32)  81.1 us
    reduce_scatter x1, waiting for transfers between devices, reduce_end(): lax.psum_scatter(grads[10].astype(jnp.bfloat16), 'band', scatter_dimensio...  50.4 us
    reduce_scatter x1, waiting for transfers between devices, reduce_end(): lax.psum_scatter(grads[8].astype(jnp.bfloat16), 'band', scatter_dimension...  50.4 us
    while x144, local copies, waits for them, and re-layouts  49.5 us
    unnamed x193, local copies, waits for them, and re-layouts  47.8 us
  transfers between devices with their start and end apart: 17, of which 9 were waited for; matrix products, arithmetic and copies ran while one was open for 43% of the time, Pallas kernels for 0%

commit v1 on v0

--- a/solution.py
+++ b/solution.py
@@ -268,7 +268,7 @@
         ).astype(jnp.float32),
     )
     return (
-        lax.psum(shares[0].astype(jnp.bfloat16), "dp").astype(jnp.float32),
+        jnp.sum(lax.all_gather(shares[0].astype(jnp.bfloat16), "dp"), axis=0).astype(jnp.float32),
         lax.psum(shares[1].astype(jnp.bfloat16), "dp").astype(jnp.float32),
         lax.psum(shares[2].astype(jnp.bfloat16), "dp").astype(jnp.float32),
         lax.psum(shares[3].astype(jnp.bfloat16), "dp").astype(jnp.float32),

time: 1110 us -> 1110 us (level)
    unnamed x2 -> x3, blocking collectives: 24 us -> 47.8 us
    psum x1 -> x0, blocking collectives: 23.1 us -> none  [reduce_end(): lax.psum(shares[0].astype(jnp.bfloat16), 'dp').astype(jnp.float32)]
    unnamed x193 -> x198, local copies, waits for them, and re-layouts: 47.8 us -> 49 us
  transfers between devices with their start and end apart: 17 -> 17, of which waited for: 9 -> 8; matrix products, arithmetic and copies ran while one was open for 43% -> 43% of each run, Pallas kernels for 0% -> 0%
where the time goes in v1:
time: 1110 us; the launch traced here: 1100 us
  matrix products  508 us (46%)
  waiting for transfers between devices  300 us (27%)
  local copies, waits for them, and re-layouts  148 us (13%)
  other arithmetic  61.3 us (6%)
  blocking collectives  58.4 us (5%)
  between operations  18.7 us (2%)
    dot_general x80, matrix products, col_dot(): lax.dot_general(left, right, (((1,), (1,)), ((), ())), preferred_element_...  197 us
    dot_general x56, matrix products, inner_dot(): return jnp.dot(left, right, preferred_element_type=jnp.float32)  184 us
    dot_general x56, matrix products, row_dot(): lax.dot_general(left, right, (((0,), (0,)), ((), ())), preferred_element_...  126 us
    psum x1, waiting for transfers between devices, reduce_end(): lax.psum(shares[2].astype(jnp.bfloat16), 'dp').astype(jnp.float32)  80.3 us
    reduce_scatter x1, waiting for transfers between devices, reduce_end(): lax.psum_scatter(grads[8].astype(jnp.bfloat16), 'band', scatter_dimension...  50.4 us
    reduce_scatter x1, waiting for transfers between devices, reduce_end(): lax.psum_scatter(grads[10].astype(jnp.bfloat16), 'band', scatter_dimensio...  49.8 us
    while x144, local copies, waits for them, and re-layouts  49.3 us
    unnamed x198, local copies, waits for them, and re-layouts  49 us
  transfers between devices with their start and end apart: 17, of which 8 were waited for; matrix products, arithmetic and copies ran while one was open for 43% of the time, Pallas kernels for 0%

profile of v1, /device:TPU:0, one launch (start us, length us, event | category | flops | bytes accessed | tf_op | source)
XLA Modules:
  0.0 1097.1 jit_solution(10220737343310803131)
XLA Ops:
  14.2 13.5 %all-reduce.18 = (bf16[768]{0:T(1024)(128)(2,1)S(1)}, bf16[768]{0:T(1024)(128)(2,1)S(1)}, bf16[768]{0:T(1024)(128)(2,1)S(1)}, bf16[768]{0:T(1024)(128)(2,1)S(1)}, bf16[768]{0:T(1024)(128)(2,1)S(1)}) all-reduce(bf16[768]{0:T(1024)(128)(2,1)S(1)} %dynamic-update-slice.1, ...), channel_id=1, replica_groups=mesh['dp'=8,'band'=4] {'band'}, use_global_device_ids=true, to_apply=%add.1 | all-reduce | flops 3840 | bytes 15360
  74.0 7.5 all-gather.26.cloned.1.call-done
  86.3 6.7 copy.98
  93.0 19.2 %all-gather.24.cloned.1.call-done = bf16[2048,768]{1,0:T(8,128)(2,1)} async-done(((bf16[512,768]{1,0:T(8,128)(2,1)}), bf16[2048,768]{1,0:T(8,128)(2,1)}) %all-gather.24.cloned.1.call-update) | async-done | bytes 3145744 | tf_op jit(solution)/shard_map/all_gather | solution.py:142
  116.9 6.7 copy.97
  124.6 104.6 %while.51 = (s32[]{:T(128)}, bf16[12,512,64]{1,2,0:T(8,128)(2,1)}, f32[12,512]{1,0:T(8,128)S(1)}, s32[1,1,512]{2,1,0:T(1,128)S(1)}, bf16[12,512,64]{2,1,0:T(8,12...) while((s32[]{:T(128)}, bf16[12,512,64]{1,2,0:T(8,128)(2,1)}, ...), condition=%wide.region_13.14_spmd.clone, body=%wide.region_10.13_spmd.clone.sunk | while | flops 277872128 | bytes 30730372 | solution.py:72
  252.7 97.3 %while.50 = (s32[]{:T(128)}, bf16[12,512,64]{1,2,0:T(8,128)(2,1)S(1)}, f32[12,512]{1,0:T(8,128)S(1)}, s32[1,1,512]{2,1,0:T(1,128)S(1)}, bf16[12,512,64]{2,1,0:T(...) while((s32[]{:T(128)}, ...), condition=%wide.region_5.6_spmd.clone, body=%wide.region_2.5_spmd.clone.sunk | while | flops 277872128 | bytes 30730372 | solution.py:72
  356.2 7.3 fusion.171
  368.4 9.7 convert_reduce_fusion.1
  384.9 8.8 convert_reduce_fusion
  407.7 130.5 %while.52 = (s32[]{:T(128)}, bf16[12,512,64]{1,2,0:T(8,128)(2,1)}, bf16[12,2048,64]{1,2,0:T(8,128)(2,1)S(1)}, bf16[12,2048,64]{1,2,0:T(8,128)(2,1)}, s32[1,1,512...) while((s32[]{:T(128)}, bf16[12,512,64]{1,2,0:T(8,128)(2,1)}, ...), condition=%wide.region_20.21_spmd.clone, body=%wide.region_18.20_spmd.clone.sunk | while | flops 681737728 | bytes 34655352 | solution.py:106
  548.4 139.2 %while.53 = (s32[]{:T(128)}, bf16[12,512,64]{1,2,0:T(8,128)(2,1)}, bf16[12,2048,64]{1,2,0:T(8,128)(2,1)S(1)}, bf16[12,2048,64]{1,2,0:T(8,128)(2,1)}, s32[1,1,512...) while((s32[]{:T(128)}, bf16[12,512,64]{1,2,0:T(8,128)(2,1)}, ...), condition=%wide.region_29.30_spmd.clone, body=%wide.region_27.29_spmd.clone.sunk | while | flops 681737728 | bytes 34655352 | solution.py:106
  699.7 9.0 add_convert_fusion
  721.0 6.9 fusion.135
  727.9 39.5 %reduce-scatter.15.cloned.1.call-done = bf16[512,768]{0,1:T(8,128)(2,1)} async-done(((bf16[2048,768]{0,1:T(8,128)(2,1)}), bf16[512,768]{0,1:T(8,128)(2,1)}) %reduce-scatter.15.cloned.1.call-update) | async-done | bytes 786448 | tf_op jit(solution)/shard_map/reduce_scatter | solution.py:181
  767.4 7.9 add_convert_fusion.2
  796.8 49.8 %reduce-scatter.23.cloned.1.call-done = bf16[768,768]{1,0:T(8,128)(2,1)} async-done(((bf16[3072,768]{1,0:T(8,128)(2,1)}), bf16[768,768]{1,0:T(8,128)(2,1)}) %reduce-scatter.23.cloned.1.call-update) | async-done | bytes 1179664 | tf_op jit(solution)/shard_map/reduce_scatter | solution.py:263
  846.6 50.4 %reduce-scatter.21.cloned.1.call-done = bf16[192,3072]{1,0:T(8,128)(2,1)} async-done(((bf16[768,3072]{1,0:T(8,128)(2,1)}), bf16[192,3072]{1,0:T(8,128)(2,1)}) %reduce-scatter.21.cloned.1.call-update) | async-done | bytes 1179664 | tf_op jit(solution)/shard_map/reduce_scatter | solution.py:257
  897.0 42.8 %reduce-scatter.17.cloned.1.call-done = bf16[192,2304]{1,0:T(8,128)(2,1)} async-done(((bf16[768,2304]{1,0:T(8,128)(2,1)}), bf16[192,2304]{1,0:T(8,128)(2,1)}) %reduce-scatter.17.cloned.1.call-update) | async-done | bytes 884752 | tf_op jit(solution)/shard_map/reduce_scatter | solution.py:239
  941.2 10.5 all-reduce.17
  952.5 23.8 %all-reduce.15 = (bf16[1536]{0:T(1024)(128)(2,1)S(1)}, bf16[192]{0:T(256)(128)(2,1)S(1)}, bf16[384]{0:T(512)(128)(2,1)S(1)}, bf16[192]{0:T(256)(128)(2,1)S(1)}, ...) all-reduce(bf16[1536]{0:T(1024)(128)(2,1)S(1)} %dynamic-update-slic, ...), channel_id=2, replica_groups=mesh['dp'=8,'band'=4] {'dp'}, use_global_device_ids=true, to_apply=%add.6 | all-reduce | flops 3648 | bytes 14592
  985.2 8.3 fusion.132
  993.6 8.4 fusion.133
  1003.3 80.3 %all-reduce.21.cloned.1.call-done = (bf16[192,2304]{1,0:T(8,128)(2,1)}, bf16[192,768]{1,0:T(8,128)(2,1)}, bf16[192,3072]{1,0:T(8,128)(2,1)}, bf16[768,768]{1,0:T(8,128)(2,1)}) async-done(((bf16[192,2304]{1,0:T(8,128)(2,1)}, bf16[192,768]{1,0:T(8,128)(2,1)}, bf16[192,3072]{1,0:T(8,128)(2,1)}, bf16[768,768]{1,0:T(8,128)(2,1)}), (bf16[192,2304]{1,0:T(8,128)(2,1)}, bf16[192,768]{1,0:T(8,128)(2,1)}, ...) | async-done | bytes 3538960 | tf_op jit(solution)/shard_map/psum | solution.py:273
  (780 shorter events, 659.7 us)
Async XLA Ops:
  7.2 28.2 %copy-start.2 = (bf16[2,1,512,768]{3,2,1,0:T(8,128)(2,1)S(1)}, bf16[2,1,512,768]{3,2,1,0:T(8,128)(2,1)}, u32[]{:S(2)}) copy-start(bf16[2,1,512,768]{3,2,1,0:T(8,128)(2,1)} %param.23) | copy-start | bytes 4718596
  7.2 36.0 %all-gather.12.cloned.1.call-start = ((), (), s32[]{:S(2)}) async-start(), calls=%async_computation.8 | async-start | bytes 4423680 | tf_op jit(solution)/shard_map/all_gather | solution.py:218
  7.9 73.6 %all-gather.26.cloned.1.call-start = ((), (), s32[]{:S(2)}) async-start(), calls=%async_computation.15 | async-start | bytes 3932160 | tf_op jit(solution)/shard_map/all_gather | solution.py:143
  52.7 59.5 %all-gather.24.cloned.1.call-start = ((), (), s32[]{:S(2)}) async-start(), calls=%async_computation.14 | async-start | bytes 3932160 | tf_op jit(solution)/shard_map/all_gather | solution.py:142
  55.2 174.0 %all-gather.16.cloned.1.call-start = ((), (), s32[]{:S(2)}) async-start(), calls=%async_computation.10 | async-start | bytes 3932160 | tf_op jit(solution)/shard_map/all_gather | solution.py:143
  55.8 185.4 %all-gather.14.cloned.1.call-start = ((), (), s32[]{:S(2)}) async-start(), calls=%async_computation.9 | async-start | bytes 3932160 | tf_op jit(solution)/shard_map/all_gather | solution.py:142
  58.2 291.7 %all-gather.18.cloned.1.call-start = ((), (), s32[]{:S(2)}) async-start(), calls=%async_computation.11 | async-start | bytes 1474560 | tf_op jit(solution)/shard_map/all_gather | solution.py:220
  58.8 297.3 %all-gather.20.cloned.1.call-start = ((), (), s32[]{:S(2)}) async-start(), calls=%async_computation.12 | async-start | bytes 5898240 | tf_op jit(solution)/shard_map/all_gather | solution.py:224
  59.6 308.9 %all-gather.22.cloned.1.call-start = ((), (), s32[]{:S(2)}) async-start(), calls=%async_computation.13 | async-start | bytes 5898240 | tf_op jit(solution)/shard_map/all_gather | solution.py:226
  60.3 659.6 %reduce-scatter.11.cloned.1.call-start = ((), (), s32[]{:S(2)}) async-start(), calls=%async_computation.17 | async-start | bytes 3932160 | tf_op jit(solution)/shard_map/reduce_scatter | solution.py:181
  60.4 303.0 %copy-start.62 = (f32[768]{0:T(1024)}, f32[768]{0:T(1024)S(1)}, u32[]{:S(2)}) copy-start(f32[768]{0:T(1024)S(1)} %convert_element_type.391) | copy-start | bytes 9220
  353.4 44.1 %copy-start.13 = (f32[512,768]{1,0:T(8,128)}, f32[512,768]{1,0:T(8,128)S(1)}, u32[]{:S(2)}) copy-start(f32[512,768]{1,0:T(8,128)S(1)} %get-tuple-element.761) | copy-start | bytes 4718596
  538.2 181.6 %reduce-scatter.9.cloned.1.call-start = ((), (), s32[]{:S(2)}) async-start(), calls=%async_computation.16 | async-start | bytes 3932160 | tf_op jit(solution)/shard_map/reduce_scatter | solution.py:178
  544.9 183.0 %reduce-scatter.13.cloned.1.call-start = ((), (), s32[]{:S(2)}) async-start(), calls=%async_computation.18 | async-start | bytes 3932160 | tf_op jit(solution)/shard_map/reduce_scatter | solution.py:178
  689.3 78.1 %reduce-scatter.15.cloned.1.call-start = ((), (), s32[]{:S(2)}) async-start(), calls=%async_computation.19 | async-start | bytes 3932160 | tf_op jit(solution)/shard_map/reduce_scatter | solution.py:181
  689.9 106.8 %reduce-scatter.19.cloned.1.call-start = ((), (), s32[]{:S(2)}) async-start(), calls=%async_computation.21 | async-start | bytes 1474560 | tf_op jit(solution)/shard_map/reduce_scatter | solution.py:245
  693.3 153.3 %reduce-scatter.23.cloned.1.call-start = ((), (), s32[]{:S(2)}) async-start(), calls=%async_computation.23 | async-start | bytes 5898240 | tf_op jit(solution)/shard_map/reduce_scatter | solution.py:263
  708.7 188.3 %reduce-scatter.21.cloned.1.call-start = ((), (), s32[]{:S(2)}) async-start(), calls=%async_computation.22 | async-start | bytes 5898240 | tf_op jit(solution)/shard_map/reduce_scatter | solution.py:257
  719.6 220.2 %reduce-scatter.17.cloned.1.call-start = ((), (), s32[]{:S(2)}) async-start(), calls=%async_computation.20 | async-start | bytes 4423680 | tf_op jit(solution)/shard_map/reduce_scatter | solution.py:239
  721.0 46.4 %copy-start.41 = (f32[512]{0:T(512)S(1)}, f32[512]{0:T(512)}, u32[]{:S(2)}) copy-start(f32[512]{0:T(512)} %copy-done.40) | copy-start | bytes 6148
  721.0 46.4 %copy-start.45 = (f32[512]{0:T(512)S(1)}, f32[512]{0:T(512)}, u32[]{:S(2)}) copy-start(f32[512]{0:T(512)} %copy-done.44) | copy-start | bytes 6148
  775.4 308.2 %all-reduce.21.cloned.1.call-start = ((), (), s32[]{:S(2)}) async-start(), calls=%async_computation.24 | async-start | bytes 7077888 | tf_op jit(solution)/shard_map/psum | solution.py:273
  796.7 184.3 %copy-start.5 = (f32[512,768]{1,0:T(8,128)S(1)}, f32[512,768]{1,0:T(8,128)}, u32[]{:S(2)}) copy-start(f32[512,768]{1,0:T(8,128)} %copy-done.4) | copy-start | bytes 4718596
  796.7 184.3 %copy-start.49 = (f32[512]{0:T(512)S(1)}, f32[512]{0:T(512)}, u32[]{:S(2)}) copy-start(f32[512]{0:T(512)} %copy-done.48) | copy-start | bytes 6148
  (100 other events, 414.3 us)
Sparse Core Ops, SparseCore 0:
  9.6 33.6 all-gather.11
  52.8 28.6 all-gather.25
  83.6 28.4 all-gather.23
  114.2 28.4 all-gather.15
  144.1 28.4 all-gather.13
  174.1 17.4 all-gather.17
  193.1 37.4 all-gather.19
  232.1 37.4 all-gather.21
  538.4 37.8 reduce-scatter.10
  578.6 37.7 reduce-scatter.8
  689.4 37.8 reduce-scatter.12
  729.7 37.7 reduce-scatter.14
  770.6 25.6 reduce-scatter.18
  798.6 47.9 reduce-scatter.22
  849.0 47.9 reduce-scatter.20
  899.4 40.3 reduce-scatter.16
  943.6 139.8 all-reduce.20
